TPU v7x, 256 devices: a whole 4x4x8 slice. The times are simulated.
256 devices in a mesh: ctx: 8 (over z), head: 32 (over y, x, core).
Axes of the slice: x: 4, y: 4, z: 8, core: 2. Of those that a mesh axis runs over, the one named last changes fastest.
Arguments:
- x_stream: bfloat16 [32768, 16384], P('ctx', 'head'), may hold values from -6 to 6
- gate_z: bfloat16 [32768, 16384], P('ctx', 'head'), as said below
- state_proj: bfloat16 [32768, 2048], P('ctx', 'head'), may hold values from -5 to 5
- dt_raw: float32 [32768, 256], P('ctx', 'head'), as said below
- dt_bias: float32 [256], P('head'), may hold values from -3 to -1
- a_log: float32 [256], P('head'), as said below
- skip_d: float32 [256], P('head'), may hold values from 0.5 to 1.5
- conv_x: bfloat16 [4, 16384], P(None, 'head'), may hold values from -3 to 3
- conv_proj: bfloat16 [4, 2048], P(None, 'head'), may hold values from -3 to 3
- norm_gain: float32 [16384], P('head'), may hold values from 0.5 to 1.5
Outputs:
- mixer_out: bfloat16 [32768, 16384], P('ctx', 'head')
Inputs may be any that keep to these rules, and one draw needn't show every extreme that they name: gate_z is a bounded normal draw whose scale varies by column. dt_raw is bounded; its level varies over blocks of 4096 tokens and heads. a_log is finite.
All inputs are finite; a program needn't handle non-finite values.
Results may differ from a plain program's by a relative error of at most 0.0085.
Values may be sent and summed in bfloat16 or wider, within the bound.
No kernel may reach another device: no remote copies, remote signals or barrier semaphores. Data moves between devices by JAX's collectives and lax.ppermute only.
A program may use at most 128 MiB of HBM per device.

v0:
```python
import jax
import jax.numpy as jnp
from jax import lax
from jax.sharding import PartitionSpec as P

HEADS = 256
STATE = 128
GROUPS = 8
BLOCK_LEN = 128


def passed_along(x, axis, by):
    count = lax.axis_size(axis)
    pairs = [(i, i + by) for i in range(count) if 0 <= i + by < count]
    return lax.ppermute(x, axis, pairs)


def swapped(value, axis, bit):
    mask = 2**bit
    pairs = [(source, source ^ mask) for source in range(lax.axis_size(axis))]
    return lax.ppermute(value, axis, pairs)


def conv_silu(sequence, edge_rows, weight):
    kernel_len = weight.shape[0]
    length = sequence.shape[0]
    padded = jnp.concatenate([edge_rows, sequence], axis=0).astype(jnp.float32)
    weight_wide = weight.astype(jnp.float32)
    total = jnp.zeros(sequence.shape, jnp.float32)
    for offset in range(kernel_len):
        total = total + weight_wide[offset] * padded[offset : offset + length]
    return jax.nn.silu(total).astype(jnp.bfloat16)


def join_pair(mine, other, upper):
    return jnp.where(
        upper, jnp.concatenate([other, mine], axis=1), jnp.concatenate([mine, other], axis=1)
    )


def block_scan(x_blocks, b_blocks, c_blocks, step_size, log_decay):
    highest = lax.Precision.HIGHEST
    running = jnp.cumsum(jnp.swapaxes(log_decay, 1, 2), axis=2)
    step_heads = jnp.swapaxes(step_size, 1, 2)
    gram_matrix = jnp.einsum("ctn,csn->cts", c_blocks, b_blocks, preferred_element_type=jnp.float32)
    block_len = running.shape[2]
    row_ids = jnp.arange(block_len)[:, None]
    col_ids = jnp.arange(block_len)[None, :]
    causal_mask = row_ids >= col_ids
    log_gaps = running[:, :, :, None] - running[:, :, None, :]
    decay_matrix = jnp.where(causal_mask, jnp.exp(jnp.where(causal_mask, log_gaps, 0.0)), 0.0)
    weights = (gram_matrix[:, None] * decay_matrix * step_heads[:, :, None, :]).astype(jnp.bfloat16)
    intra_out = jnp.einsum("chts,cshp->cthp", weights, x_blocks, preferred_element_type=jnp.float32)
    block_total = running[:, :, -1]
    state_weight = jnp.exp(block_total[:, :, None] - running) * step_heads
    weighted = (x_blocks.astype(jnp.float32) * jnp.swapaxes(state_weight, 1, 2)[..., None]).astype(
        jnp.bfloat16
    )
    states = jnp.einsum("cshp,csn->chpn", weighted, b_blocks, preferred_element_type=jnp.float32)

    def advance(state_now, inputs):
        factor, addend = inputs
        return (factor[:, None, None] * state_now + addend, state_now)

    empty_state = jnp.zeros(states.shape[1:], jnp.float32)
    final_state, entering = lax.scan(advance, empty_state, (jnp.exp(block_total), states))
    c_wide = c_blocks.astype(jnp.float32)
    inter_out = jnp.exp(jnp.swapaxes(running, 1, 2))[..., None] * jnp.einsum(
        "ctn,chpn->cthp", c_wide, entering, precision=highest
    )
    return (intra_out + inter_out, final_state, block_total, running)


def on_device(
    x_stream, gate_z, state_proj, dt_raw, dt_bias, a_log, skip_d, conv_x, conv_proj, norm_gain
):
    highest = lax.Precision.HIGHEST
    kernel_len = conv_x.shape[0]
    tokens_here = x_stream.shape[0]
    heads_here = dt_raw.shape[1]
    channels = x_stream.shape[1]
    head_size = channels // heads_here
    head_pos = lax.axis_index("head")
    group_devices = lax.axis_size("head") // GROUPS
    group_levels = group_devices.bit_length() - 1
    edge_start = tokens_here - kernel_len + 1
    edge_rows = passed_along((x_stream[edge_start:], state_proj[edge_start:]), "ctx", 1)
    x_conv = conv_silu(x_stream, edge_rows[0], conv_x)
    own_cols = conv_silu(state_proj, edge_rows[1], conv_proj)
    for level in range(group_levels):
        upper = head_pos >> level & 1 == 1
        other_cols = swapped(own_cols, "head", level)
        own_cols = join_pair(own_cols, other_cols, upper)
    blocks = tokens_here // BLOCK_LEN
    b_blocks = own_cols[:, :STATE].reshape(blocks, BLOCK_LEN, STATE)
    c_blocks = own_cols[:, STATE:].reshape(blocks, BLOCK_LEN, STATE)
    step_size = jax.nn.softplus(dt_raw + dt_bias)
    log_decay = step_size * -jnp.exp(a_log)
    local_out, final_state, block_total, running = block_scan(
        x_conv.reshape(blocks, BLOCK_LEN, heads_here, head_size),
        b_blocks,
        c_blocks,
        step_size.reshape(blocks, BLOCK_LEN, heads_here),
        log_decay.reshape(blocks, BLOCK_LEN, heads_here),
    )
    block_log = jnp.sum(block_total, axis=0)
    block_logs = lax.all_gather(block_log[None], "ctx", axis=0, tiled=True)
    ctx_pos = lax.axis_index("ctx")
    count = block_logs.shape[0]
    indices = jnp.arange(count)
    between = (indices[None, :] > indices[:, None]) & (indices[None, :] < ctx_pos)
    span_logs = jnp.dot(between.astype(jnp.float32), block_logs, precision=highest)
    weight_all = jnp.where(indices[:, None] < ctx_pos, jnp.exp(span_logs), 0.0)
    entering = jnp.zeros(final_state.shape, jnp.float32) + jnp.einsum(
        "rh,rhpn->hpn",
        weight_all,
        lax.all_gather(final_state[None].astype(jnp.bfloat16), "ctx", axis=0, tiled=True).astype(
            jnp.float32
        ),
        precision=highest,
    )
    block_start = jnp.cumsum(block_total, axis=0) - block_total
    carried_out = jnp.exp(jnp.swapaxes(running + block_start[:, :, None], 1, 2))[
        ..., None
    ] * jnp.einsum("ctn,hpn->cthp", c_blocks.astype(jnp.float32), entering, precision=highest)
    mixed = (local_out + carried_out).reshape(tokens_here, heads_here, head_size)
    mixed = mixed + skip_d[None, :, None] * x_conv.astype(jnp.float32).reshape(
        tokens_here, heads_here, head_size
    )
    gated_out = mixed.reshape(tokens_here, channels) * jax.nn.silu(gate_z.astype(jnp.float32))
    group_total = jnp.sum(gated_out * gated_out, axis=1)
    for level in range(group_levels):
        group_total = group_total + swapped(group_total, "head", level)
    mean_square = group_total / (HEADS // GROUPS * head_size)
    normed = gated_out * lax.rsqrt(mean_square + 1e-05)[:, None] * norm_gain[None, :]
    return normed.astype(jnp.bfloat16)


def solution(mesh):
    return jax.shard_map(
        on_device,
        mesh=mesh,
        in_specs=(
            P("ctx", "head"),
            P("ctx", "head"),
            P("ctx", "head"),
            P("ctx", "head"),
            P("head"),
            P("head"),
            P("head"),
            P(None, "head"),
            P(None, "head"),
            P("head"),
        ),
        out_specs=P("ctx", "head"),
        check_vma=False,
    )
```

profile of v0, /device:TPU:2, one launch (start us, length us, event | category | flops | bytes accessed | tf_op | source)
XLA Modules:
  0.0 275.4 jit_solution(6585836205751092210)
XLA Ops:
  7.5 3.8 %collective-permute-start.1 = (bf16[3,64]{0,1:T(8,128)(2,1)S(1)}, bf16[3,64]{0,1:T(8,128)(2,1)S(1)}, u32[]{:S(2)}, u32[]{:S(2)}) collective-permute-start(bf16[3,64]{0,1:T(8,128)(2,1)S(1)} %slice.73), channel_id=1, source_target_pairs={{0,32},{32,64},{64,96},{96,128},{128,160},{160,192},{192,224},{1,3... | collective-permute-start | bytes 1160 | tf_op jit(solution)/shard_map/ppermute | solution.py:15
  12.2 3.8 %collective-permute-start = (bf16[3,512]{0,1:T(8,128)(2,1)S(1)}, bf16[3,512]{0,1:T(8,128)(2,1)S(1)}, u32[]{:S(2)}, u32[]{:S(2)}) collective-permute-start(bf16[3,512]{0,1:T(8,128)(2,1)S(1)} %copy.30), channel_id=1, source_target_pairs={{0,32},{32,64},{64,96},{96,128},{128,160},{160,192},{192,224},{1,3... | collective-permute-start | bytes 9224 | tf_op jit(solution)/shard_map/ppermute | solution.py:15
  16.0 6.5 %copy.31 = bf16[4096,512]{0,1:T(8,128)(2,1)} copy(bf16[4096,512]{1,0:T(8,128)(2,1)} %param.12) | data formatting | bytes 8388608 | tf_op args[0]
  23.4 9.0 %reduce_window_sum.22 = f32[32,8,128]{2,1,0:T(8,128)S(1)} reduce-window(f32[32,8,128]{2,1,0:T(8,128)S(1)} %get-tuple-element.77, f32[]{:T(128)} %constant.42.clone.1), window={size=1x1x128 pad=0_0x0_0x127_0}, to_apply=%region_0.1 | reduce-window | flops 4161536 | bytes 262148 | tf_op jit(solution)/shard_map/jit(cumsum)/reduce_window_sum | solution.py:43
  35.5 17.0 %all-reduce = f32[64]{0:T(128)S(1)} all-reduce(f32[64]{0:T(128)S(1)} %dynamic-update-slice), channel_id=2, replica_groups=mesh['ctx'=8,'head'=32] {'ctx'}, use_global_device_ids=true, to_apply=%add | all-reduce | flops 64 | bytes 512
  55.1 6.3 %copy.43 = bf16[4096,512]{0,1:T(8,128)(2,1)} copy(bf16[4096,512]{1,0:T(8,128)(2,1)} %param.13) | data formatting | bytes 8388608 | tf_op args[1]
  64.3 2.5 maximum_convert_fusion
  67.8 8.7 %fusion.46 = bf16[64,8,32,128]{3,1,2,0:T(8,128)(2,1)} fusion(f32[4099,512]{0,1:T(8,128)S(1)} %maximum_convert_fusion, f32[512]{0:T(512)S(1)} %bitcast.109, f32[512]{0:T(512)S(1)} %bitcast.107, f32[512]{0:T(512)S(1)} %bitcast.105, f32[512]{0:T(512)S(1)} %bitcast.103), kind=kLoop, calls=%fused_computation.78 | loop fusion | flops 25165824 | bytes 37756928
  76.5 3.4 %copy.52 = bf16[64,8,32,128]{3,2,1,0:T(8,128)(2,1)S(1)} copy(bf16[64,8,32,128]{3,1,2,0:T(8,128)(2,1)} %fusion.46) | data formatting | bytes 8388608
  79.9 3.2 %multiply_convert_fusion.3 = bf16[32,128,8,64]{1,0,3,2:T(8,128)(2,1)} fusion(bf16[32,128,8,64]{1,0,3,2:T(8,128)(2,1)S(1)} %bitcast.95, f32[32,128,8]{1,0,2:T(8,128)S(1)} %copy.37), kind=kLoop, calls=%fused_computation.24 | loop fusion | flops 6291456 | bytes 8519680 | tf_op jit(solution)/shard_map/convert_element_type | solution.py:56
  83.2 8.8 %collective-permute-done.3 = bf16[4096,128]{0,1:T(8,128)(2,1)S(1)} collective-permute-done((bf16[4096,128]{0,1:T(8,128)(2,1)S(1)}, bf16[4096,128]{0,1:T(8,128)(2,1)S(1)}, u32[]{:S(2)}, u32[]{:S(2)}) %collective-permute-start.3) | collective-permute-done | bytes 1048608 | tf_op jit(solution)/shard_map/ppermute | solution.py:21
  93.3 7.6 %fusion.16 = f32[32,8,64,128]{3,2,1,0:T(8,128)} fusion(bf16[32,128,128,1]{2,1,3,0:T(8,128)(2,1)S(1)} %bitcast.97, bf16[32,128,8,64]{1,0,3,2:T(8,128)(2,1)} %multiply_convert_fusion.3), kind=kOutput, calls=%fused_computation.33 | convolution fusion | flops 536870912 | bytes 13631488 | tf_op jit(solution)/shard_map/cshp,csn->chpn/dot_general | solution.py:59
  100.9 79.2 %while.13 = (s32[]{:T(128)}, f32[8,64,128]{2,1,0:T(8,128)S(1)}, f32[32,8,64,128]{3,2,1,0:T(8,128)}, f32[32,8]{1,0:T(8,128)}, f32[32,8,64,128]{3,2,1,0:T(8,128)}, /*index=5*/s32[]{:T(128)}, s32[]{:T(128)}) while((s32[]{:T(128)}, f32[8,64,128]{2,1,0:T(8,128)S(1)}, f32[32,8,64,128]{3,2,1,0:T(8,128)}, f32[32,8]{1,0:T(8,128)}, ...), condition=%wide.region_2.3_spmd.clone, body=%wide.region_1.2_spmd.clone.sunk | while | flops 262147 | bytes 1311424 | solution.py:66
  182.3 8.4 %fusion.36 = f32[32,128,8,64]{1,3,2,0:T(8,128)} fusion(bf16[32,128,128,1]{2,1,3,0:T(8,128)(2,1)S(1)} %bitcast.93, f32[32,8,64,128]{3,2,1,0:T(8,128)} %get-tuple-element.33), kind=kOutput, calls=%fused_computation.77 | convolution fusion | flops 3221225472 | bytes 17825792 | tf_op jit(solution)/shard_map/ctn,chpn->cthp/dot_general | solution.py:68
  190.7 10.7 %fusion.1 = f32[32,8,64,128]{3,2,1,0:T(8,128)} fusion(f32[32,8,128]{2,1,0:T(8,128)S(1)} %copy-done.9, f32[32,8,128]{2,1,0:T(8,128)S(1)} %reduce_window_sum.22, f32[32,128,128]{2,1,0:T(8,128)S(1)} %fusion.35, pred[128,128]{1,0:T(8,128)(4,1)S(1)} %copy-done.11, bf16[32,128,8,64]{1,0,3,2:T(8,128)(2,1)S(1)} %bitcast.96), kind=kOutput, calls=%fused_computation.7 | convolution fusion | flops 562036736 | bytes 14958592 | tf_op jit(solution)/shard_map/chts,cshp->cthp/dot_general | solution.py:53
  201.4 19.5 %all-gather.4.cloned.1.call-done = bf16[64,64,128]{2,1,0:T(8,128)(2,1)} async-done(((bf16[8,64,128]{2,1,0:T(8,128)(2,1)}), bf16[64,64,128]{2,1,0:T(8,128)(2,1)}) %all-gather.4.cloned.1.call-update) | async-done | bytes 1048592 | tf_op jit(solution)/shard_map/all_gather | solution.py:117
  220.9 2.5 fusion.24
  223.5 8.3 %fusion.9 = f32[32,128,8,64]{1,3,2,0:T(8,128)S(1)} fusion(f32[32,8,64,128]{3,2,1,0:T(8,128)} %fusion.1, f32[32,128,8,64]{1,3,2,0:T(8,128)} %fusion.36, f32[32,128,8]{1,2,0:T(8,128)S(1)} %copy-done.7, f32[32,128,8]{1,2,0:T(8,128)S(1)} %copy-done.6, bf16[32,128,128,1]{2,1,3,0:T(8,128)(2,1)S(1)} %bitcast.94, f32[8,64,128,1]{2,1,0,3:T(8,128)S(1)} %bitcast.99), kind=kOutput, calls=%fused_computation.21 | convolution fusion | flops 3229614080 | bytes 26738688 | tf_op jit(solution)/shard_map/ctn,hpn->cthp/dot_general | solution.py:125
  231.8 8.0 %copy.42 = f32[32,128,8,64]{1,0,3,2:T(8,128)} copy(f32[32,128,8,64]{1,3,2,0:T(8,128)S(1)} %fusion.9) | data formatting | bytes 16777216 | tf_op jit(solution)/shard_map/add | solution.py:126
  239.9 13.9 %multiply_reduce_fusion = (f32[4096]{0:T(1024)S(1)}, f32[4096,512]{0,1:T(8,128)S(1)}) fusion(bf16[4096,512]{0,1:T(8,128)(2,1)S(1)} %copy-done.4, f32[512]{0:T(512)S(1)} %copy-done.13, f32[64,8,32,128]{3,2,1,0:T(8,128)} %bitcast.91, f32[4099,512]{0,1:T(8,128)S(1)} %bitcast.90, f32[512]{0:T(512)S(1)} %bitcast.110, f32[512]{0:T(512)S(1)} %bitcast.108, ...), kind=kLoop, calls=%fused_computation.23 | loop fusion | flops 48230400 | bytes 54552576 | tf_op jit(solution)/shard_map/reduce_sum | solution.py:131
  253.9 1.2 collective-permute-done.4
  255.5 3.2 %collective-permute-done.5 = f32[4096]{0:T(1024)S(1)} collective-permute-done((f32[4096]{0:T(1024)S(1)}, f32[4096]{0:T(1024)S(1)}, u32[]{:S(2)}, u32[]{:S(2)}) %collective-permute-start.5) | collective-permute-done | bytes 16416 | tf_op jit(solution)/shard_map/ppermute | solution.py:21
  258.8 3.3 %multiply_convert_fusion.2 = bf16[4096,512]{0,1:T(8,128)(2,1)} fusion(f32[4096,512]{0,1:T(8,128)S(1)} %get-tuple-element.74, f32[512]{0:T(512)S(1)} %copy-done.15, f32[4096]{0:T(1024)S(1)} %add_rsqrt_fusion), kind=kLoop, calls=%fused_computation.22 | loop fusion | flops 6291456 | bytes 12601344 | tf_op jit(solution)/shard_map/convert_element_type | solution.py:136
  262.2 6.4 %copy.44 = bf16[4096,512]{1,0:T(8,128)(2,1)} copy(bf16[4096,512]{0,1:T(8,128)(2,1)} %multiply_convert_fusion.2) | data formatting | bytes 8388608 | tf_op jit(solution)/shard_map/convert_element_type | solution.py:136
  (193 shorter events, 94.1 us)
Async XLA Ops:
  6.5 27.5 %copy-start.19 = (u32[256]{0:T(256)S(1)}, u32[256]{0:T(256)}, u32[]{:S(2)}) copy-start(u32[256]{0:T(256)} %constant.53) | copy-start | bytes 3076
  6.5 16.0 %copy-start.18 = (f32[8]{0:T(128)S(1)}, f32[8]{0:T(128)}, u32[]{:S(2)}) copy-start(f32[8]{0:T(128)} %param.17) | copy-start | bytes 100
  6.5 16.0 %copy-start.8 = (f32[4096,8]{0,1:T(8,128)S(1)}, f32[4096,8]{0,1:T(8,128)}, u32[]{:S(2)}) copy-start(f32[4096,8]{0,1:T(8,128)} %param.15) | copy-start | bytes 393220
  6.5 16.0 %copy-start.14 = (f32[8]{0:T(128)S(1)}, f32[8]{0:T(128)}, u32[]{:S(2)}) copy-start(f32[8]{0:T(128)} %param.16) | copy-start | bytes 100
  6.5 27.2 %copy-start.16 = (bf16[4,64]{1,0:T(4,128)(2,1)S(1)}, bf16[4,64]{1,0:T(4,128)(2,1)}, u32[]{:S(2)}) copy-start(bf16[4,64]{1,0:T(4,128)(2,1)} %param.20) | copy-start | bytes 1540
  6.5 27.2 %copy-start.12 = (bf16[4,512]{1,0:T(4,128)(2,1)S(1)}, bf16[4,512]{1,0:T(4,128)(2,1)}, u32[]{:S(2)}) copy-start(bf16[4,512]{1,0:T(4,128)(2,1)} %param.19) | copy-start | bytes 12292
  6.6 214.3 %all-gather.4.cloned.1.call-start = ((), (), s32[]{:S(2)}) async-start(), calls=%async_computation | async-start | bytes 1179648 | tf_op jit(solution)/shard_map/all_gather | solution.py:117
  7.5 54.6 %collective-permute-start.1 = (bf16[3,64]{0,1:T(8,128)(2,1)S(1)}, bf16[3,64]{0,1:T(8,128)(2,1)S(1)}, u32[]{:S(2)}, u32[]{:S(2)}) collective-permute-start(bf16[3,64]{0,1:T(8,128)(2,1)S(1)} %slice.73), channel_id=1, source_target_pairs={{0,32},{32,64},{64,96},{96,128},{128,160},{160,192},{192,224},{1,3... | collective-permute-start | bytes 1160 | tf_op jit(solution)/shard_map/ppermute | solution.py:15
  12.2 51.2 %collective-permute-start = (bf16[3,512]{0,1:T(8,128)(2,1)S(1)}, bf16[3,512]{0,1:T(8,128)(2,1)S(1)}, u32[]{:S(2)}, u32[]{:S(2)}) collective-permute-start(bf16[3,512]{0,1:T(8,128)(2,1)S(1)} %copy.30), channel_id=1, source_target_pairs={{0,32},{32,64},{64,96},{96,128},{128,160},{160,192},{192,224},{1,3... | collective-permute-start | bytes 9224 | tf_op jit(solution)/shard_map/ppermute | solution.py:15
  16.0 45.4 %copy-start.17 = (f32[8]{0:T(128)S(1)}, f32[8]{0:T(128)}, u32[]{:S(2)}) copy-start(f32[8]{0:T(128)} %param.18) | copy-start | bytes 100
  16.0 46.1 %copy-start.5 = (bf16[4096,64]{0,1:T(8,128)(2,1)S(1)}, bf16[4096,64]{0,1:T(8,128)(2,1)}, u32[]{:S(2)}) copy-start(bf16[4096,64]{0,1:T(8,128)(2,1)} %param.14) | copy-start | bytes 1572868
  63.2 3.5 %collective-permute-start.2 = (bf16[4096,64]{0,1:T(8,128)(2,1)S(1)}, bf16[4096,64]{0,1:T(8,128)(2,1)S(1)}, u32[]{:S(2)}, u32[]{:S(2)}) collective-permute-start(bf16[4096,64]{0,1:T(8,128)(2,1)S(1)} %multiply_convert_fusion.5), channel_id=1, source_target_pairs={{0,1},{1,0},{2,3},{3,2},{4,5},{5,4},{6,7},{7,6},{8,9},{9,8},{10,11... | collective-permute-start | bytes 1572872 | tf_op jit(solution)/shard_map/ppermute | solution.py:21
  66.8 9.7 %copy-start = (f32[4099,512]{0,1:T(8,128)}, f32[4099,512]{0,1:T(8,128)S(1)}, u32[]{:S(2)}) copy-start(f32[4099,512]{0,1:T(8,128)S(1)} %maximum_convert_fusion) | copy-start | bytes 25184260
  67.0 24.9 %collective-permute-start.3 = (bf16[4096,128]{0,1:T(8,128)(2,1)S(1)}, bf16[4096,128]{0,1:T(8,128)(2,1)S(1)}, u32[]{:S(2)}, u32[]{:S(2)}) collective-permute-start(bf16[4096,128]{0,1:T(8,128)(2,1)S(1)} %maximum_select_fusion.1), channel_id=1, source_target_pairs={{0,2},{1,3},{2,0},{3,1},{4,6},{5,7},{6,4},{7,5},{8,10},{9,11},{10,... | collective-permute-start | bytes 3145736 | tf_op jit(solution)/shard_map/ppermute | solution.py:21
  79.9 12.7 %copy-start.2 = (bf16[64,8,32,128]{3,2,1,0:T(8,128)(2,1)}, bf16[64,8,32,128]{3,2,1,0:T(8,128)(2,1)S(1)}, u32[]{:S(2)}) copy-start(bf16[64,8,32,128]{3,2,1,0:T(8,128)(2,1)S(1)} %copy.52) | copy-start | bytes 12582916
  182.3 8.4 %copy-start.9 = (f32[32,8,128]{2,1,0:T(8,128)S(1)}, f32[32,8,128]{2,1,0:T(8,128)}, u32[]{:S(2)}) copy-start(f32[32,8,128]{2,1,0:T(8,128)} %get-tuple-element.78) | copy-start | bytes 393220
  190.7 30.2 %copy-start.10 = (f32[8,8,1,1]{0,2,3,1:T(1,128)S(1)}, f32[8,8,1,1]{0,2,3,1:T(1,128)}, u32[]{:S(2)}) copy-start(f32[8,8,1,1]{0,2,3,1:T(1,128)} %copy.47) | copy-start | bytes 772
  190.7 32.7 %copy-start.6 = (f32[32,128,8]{1,2,0:T(8,128)S(1)}, f32[32,128,8]{1,2,0:T(8,128)}, u32[]{:S(2)}) copy-start(f32[32,128,8]{1,2,0:T(8,128)} %get-tuple-element.81) | copy-start | bytes 393220
  190.7 32.7 %copy-start.7 = (f32[32,128,8]{1,2,0:T(8,128)S(1)}, f32[32,128,8]{1,2,0:T(8,128)}, u32[]{:S(2)}) copy-start(f32[32,128,8]{1,2,0:T(8,128)} %get-tuple-element.82) | copy-start | bytes 393220
  223.4 16.4 %slice-start = ((s8[8650752]{0:T(1024)(128)(4,1)}), s8[4194304]{0:T(1024)(128)(4,1)S(1)}, s32[]{:S(2)}) async-start(s8[8650752]{0:T(1024)(128)(4,1)} %bitcast.89), calls=%async_computation.1 | async-start | bytes 8388608
  223.4 16.4 %slice-start.1 = ((s8[8650752]{0:T(1024)(128)(4,1)}), s8[4194304]{0:T(1024)(128)(4,1)S(1)}, s32[]{:S(2)}) async-start(s8[8650752]{0:T(1024)(128)(4,1)} %bitcast.89), calls=%async_computation.2 | async-start | bytes 8388608
  239.9 18.9 %copy-start.15 = (f32[512]{0:T(512)S(1)}, f32[512]{0:T(512)}, u32[]{:S(2)}) copy-start(f32[512]{0:T(512)} %param.21) | copy-start | bytes 6148
  253.8 1.3 collective-permute-start.4
  255.1 3.7 %collective-permute-start.5 = (f32[4096]{0:T(1024)S(1)}, f32[4096]{0:T(1024)S(1)}, u32[]{:S(2)}, u32[]{:S(2)}) collective-permute-start(f32[4096]{0:T(1024)S(1)} %add.99), channel_id=1, source_target_pairs={{0,2},{1,3},{2,0},{3,1},{4,6},{5,7},{6,4},{7,5},{8,10},{9,11},{10,... | collective-permute-start | bytes 49160 | tf_op jit(solution)/shard_map/ppermute | solution.py:21
  (6 other events, 43.1 us)
Sparse Core Ops, SparseCore 0:
  181.6 39.3 all-gather.3
where the time goes:
time: 278 us; the launch traced here: 275 us
  other arithmetic  103 us (37%)
  local copies, waits for them, and re-layouts  60.3 us (22%)
  matrix products  38.5 us (14%)
  waiting for transfers between devices  32.7 us (12%)
  blocking collectives  17 us (6%)
  between operations  14.5 us (5%)
  starting transfers between devices  9.16 us (3%)
    add x32, other arithmetic, advance(): return (factor[:, None, None] * state_now + addend, state_now)  33.3 us
    dynamic_update_slice x32, other arithmetic, block_scan(): lax.scan(advance, empty_state, (jnp.exp(block_total), states))  23.4 us
    mul x32, local copies, waits for them, and re-layouts, advance(): return (factor[:, None, None] * state_now + addend, state_now)  21.8 us
    all_gather x1, waiting for transfers between devices, on_device(): lax.all_gather(final_state[None].astype(jnp.bfloat16), 'ctx', axis=0, til...  19.5 us
    unnamed x53, local copies, waits for them, and re-layouts  18.7 us
    unnamed x1, blocking collectives  17 us
    reduce_sum x1, other arithmetic, on_device(): group_total = jnp.sum(gated_out * gated_out, axis=1)  13.9 us
    ppermute x4, waiting for transfers between devices, swapped(): return lax.ppermute(value, axis, pairs)  13.2 us
  transfers between devices with their start and end apart: 7, of which 4 were waited for; matrix products, arithmetic and copies ran while one was open for 25% of the time, Pallas kernels for 0%

commit v1 on v0

--- a/solution.py
+++ b/solution.py
@@ -114,9 +114,15 @@
     entering = jnp.zeros(final_state.shape, jnp.float32) + jnp.einsum(
         "rh,rhpn->hpn",
         weight_all,
-        lax.all_gather(final_state[None].astype(jnp.bfloat16), "ctx", axis=0, tiled=True).astype(
-            jnp.float32
-        ),
+        jnp.concatenate(
+            lax.all_to_all(
+                jnp.stack([final_state[None].astype(jnp.bfloat16)] * lax.axis_size("ctx")),
+                "ctx",
+                0,
+                0,
+            ),
+            axis=0,
+        ).astype(jnp.float32),
         precision=highest,
     )
     block_start = jnp.cumsum(block_total, axis=0) - block_total

time: 278 us -> 258 us (0.928)
  between operations: 14.5 us -> 1.17 us
  waiting for transfers between devices: 32.7 us -> 20.8 us
  starting transfers between devices: 9.16 us -> 15.2 us
    all_gather x1 -> x0, waiting for transfers between devices: 19.5 us -> none  [on_device(): lax.all_gather(final_state[None].astype(jnp.bfloat16), 'ctx', axis=0, til...]
    all_to_all x0 -> x1, waiting for transfers between devices: none -> 7.62 us  [on_device(): lax.all_to_all(jnp.stack([final_state[None].astype(jnp.bfloat16)] * lax.a...]
    all_to_all x0 -> x1, starting transfers between devices: none -> 6.04 us  [on_device(): lax.all_to_all(jnp.stack([final_state[None].astype(jnp.bfloat16)] * lax.a...]
  transfers between devices with their start and end apart: 7 -> 7, of which waited for: 4 -> 4; matrix products, arithmetic and copies ran while one was open for 25% -> 27% of each run, Pallas kernels for 0% -> 0%
where the time goes in v1:
time: 258 us; the launch traced here: 256 us
  other arithmetic  102 us (40%)
  local copies, waits for them, and re-layouts  61.5 us (24%)
  matrix products  37.2 us (14%)
  waiting for transfers between devices  20.8 us (8%)
  blocking collectives  17 us (7%)
  starting transfers between devices  15.2 us (6%)
    add x32, other arithmetic, advance(): return (factor[:, None, None] * state_now + addend, state_now)  33.3 us
    dynamic_update_slice x32, other arithmetic, block_scan(): lax.scan(advance, empty_state, (jnp.exp(block_total), states))  23.2 us
    mul x32, local copies, waits for them, and re-layouts, advance(): return (factor[:, None, None] * state_now + addend, state_now)  21.8 us
    unnamed x53, local copies, waits for them, and re-layouts  18.7 us
    unnamed x1, blocking collectives  17 us
    reduce_sum x1, other arithmetic, on_device(): group_total = jnp.sum(gated_out * gated_out, axis=1)  14.2 us
    ppermute x4, waiting for transfers between devices, swapped(): return lax.ppermute(value, axis, pairs)  13.1 us
    dot_general x1, matrix products, block_scan(): jnp.einsum('chts,cshp->cthp', weights, x_blocks, preferred_element_type=j...  10.7 us
  transfers between devices with their start and end apart: 7, of which 4 were waited for; matrix products, arithmetic and copies ran while one was open for 27% of the time, Pallas kernels for 0%

profile of v1, /device:TPU:2, one launch (start us, length us, event | category | flops | bytes accessed | tf_op | source)
XLA Modules:
  0.0 255.6 jit_solution(7766891509395893741)
XLA Ops:
  0.9 3.8 %collective-permute-start.1 = (bf16[3,64]{0,1:T(8,128)(2,1)S(1)}, bf16[3,64]{0,1:T(8,128)(2,1)S(1)}, u32[]{:S(2)}, u32[]{:S(2)}) collective-permute-start(bf16[3,64]{0,1:T(8,128)(2,1)S(1)} %slice.73), channel_id=1, source_target_pairs={{0,32},{32,64},{64,96},{96,128},{128,160},{160,192},{192,224},{1,3... | collective-permute-start | bytes 1160 | tf_op jit(solution)/shard_map/ppermute | solution.py:15
  5.6 3.8 %collective-permute-start = (bf16[3,512]{0,1:T(8,128)(2,1)S(1)}, bf16[3,512]{0,1:T(8,128)(2,1)S(1)}, u32[]{:S(2)}, u32[]{:S(2)}) collective-permute-start(bf16[3,512]{0,1:T(8,128)(2,1)S(1)} %copy.15), channel_id=1, source_target_pairs={{0,32},{32,64},{64,96},{96,128},{128,160},{160,192},{192,224},{1,3... | collective-permute-start | bytes 9224 | tf_op jit(solution)/shard_map/ppermute | solution.py:15
  9.5 6.5 %copy.16 = bf16[4096,512]{0,1:T(8,128)(2,1)} copy(bf16[4096,512]{1,0:T(8,128)(2,1)} %param.12) | data formatting | bytes 8388608 | tf_op args[0]
  16.8 9.0 %reduce_window_sum.22 = f32[32,8,128]{2,1,0:T(8,128)S(1)} reduce-window(f32[32,8,128]{2,1,0:T(8,128)S(1)} %get-tuple-element.72, f32[]{:T(128)} %constant.42.clone.1), window={size=1x1x128 pad=0_0x0_0x127_0}, to_apply=%region_0.1 | reduce-window | flops 4161536 | bytes 262148 | tf_op jit(solution)/shard_map/jit(cumsum)/reduce_window_sum | solution.py:43
  29.0 17.0 %all-reduce = f32[64]{0:T(128)S(1)} all-reduce(f32[64]{0:T(128)S(1)} %dynamic-update-slice), channel_id=2, replica_groups=mesh['ctx'=8,'head'=32] {'ctx'}, use_global_device_ids=true, to_apply=%add | all-reduce | flops 64 | bytes 512
  48.5 6.3 %copy.28 = bf16[4096,512]{0,1:T(8,128)(2,1)} copy(bf16[4096,512]{1,0:T(8,128)(2,1)} %param.13) | data formatting | bytes 8388608 | tf_op args[1]
  57.7 2.5 maximum_convert_fusion
  61.3 8.7 %fusion.46 = bf16[64,8,32,128]{3,1,2,0:T(8,128)(2,1)} fusion(f32[4099,512]{0,1:T(8,128)S(1)} %maximum_convert_fusion, f32[512]{0:T(512)S(1)} %bitcast.109, f32[512]{0:T(512)S(1)} %bitcast.107, f32[512]{0:T(512)S(1)} %bitcast.105, f32[512]{0:T(512)S(1)} %bitcast.103), kind=kLoop, calls=%fused_computation.78 | loop fusion | flops 25165824 | bytes 37756928
  69.9 3.4 %copy.37 = bf16[64,8,32,128]{3,2,1,0:T(8,128)(2,1)S(1)} copy(bf16[64,8,32,128]{3,1,2,0:T(8,128)(2,1)} %fusion.46) | data formatting | bytes 8388608
  73.4 3.2 %multiply_convert_fusion.3 = bf16[32,128,8,64]{1,0,3,2:T(8,128)(2,1)} fusion(bf16[32,128,8,64]{1,0,3,2:T(8,128)(2,1)S(1)} %bitcast.95, f32[32,128,8]{1,0,2:T(8,128)S(1)} %copy.22), kind=kLoop, calls=%fused_computation.24 | loop fusion | flops 6291456 | bytes 8519680 | tf_op jit(solution)/shard_map/convert_element_type | solution.py:56
  76.6 8.8 %collective-permute-done.3 = bf16[4096,128]{0,1:T(8,128)(2,1)S(1)} collective-permute-done((bf16[4096,128]{0,1:T(8,128)(2,1)S(1)}, bf16[4096,128]{0,1:T(8,128)(2,1)S(1)}, u32[]{:S(2)}, u32[]{:S(2)}) %collective-permute-start.3) | collective-permute-done | bytes 1048608 | tf_op jit(solution)/shard_map/ppermute | solution.py:21
  86.7 7.6 %fusion.16 = f32[32,8,64,128]{3,2,1,0:T(8,128)} fusion(bf16[32,128,128,1]{2,1,3,0:T(8,128)(2,1)S(1)} %bitcast.97, bf16[32,128,8,64]{1,0,3,2:T(8,128)(2,1)} %multiply_convert_fusion.3), kind=kOutput, calls=%fused_computation.33 | convolution fusion | flops 536870912 | bytes 13631488 | tf_op jit(solution)/shard_map/cshp,csn->chpn/dot_general | solution.py:59
  94.3 79.0 %while.13 = (s32[]{:T(128)}, f32[8,64,128]{2,1,0:T(8,128)S(1)}, f32[32,8,64,128]{3,2,1,0:T(8,128)}, f32[32,8]{1,0:T(8,128)}, f32[32,8,64,128]{3,2,1,0:T(8,128)}, /*index=5*/s32[]{:T(128)}, s32[]{:T(128)}) while((s32[]{:T(128)}, f32[8,64,128]{2,1,0:T(8,128)S(1)}, f32[32,8,64,128]{3,2,1,0:T(8,128)}, f32[32,8]{1,0:T(8,128)}, ...), condition=%wide.region_2.3_spmd.clone, body=%wide.region_1.2_spmd.clone.sunk | while | flops 262147 | bytes 1311424 | solution.py:66
  175.3 6.0 %all-to-all-start = ((bf16[8,1,8,64,128]{4,3,2,1,0:T(8,128)(2,1)}), bf16[8,1,8,64,128]{4,3,2,1,0:T(8,128)(2,1)S(1)}, u32[]{:S(2)}, u32[]{:S(2)}) async-start(bf16[8,1,8,64,128]{4,3,2,1,0:T(8,128)(2,1)} %stack.2), calls=%async_computation | async-start | bytes 2097152 | tf_op jit(solution)/shard_map/all_to_all | solution.py:118
  182.2 8.4 %fusion.36 = f32[32,128,8,64]{1,3,2,0:T(8,128)} fusion(bf16[32,128,128,1]{2,1,3,0:T(8,128)(2,1)S(1)} %bitcast.93, f32[32,8,64,128]{3,2,1,0:T(8,128)} %get-tuple-element.33), kind=kOutput, calls=%fused_computation.77 | convolution fusion | flops 3221225472 | bytes 17825792 | tf_op jit(solution)/shard_map/ctn,chpn->cthp/dot_general | solution.py:68
  190.6 10.7 %fusion.1 = f32[32,8,64,128]{3,2,1,0:T(8,128)} fusion(f32[32,8,128]{2,1,0:T(8,128)S(1)} %copy-done.9, f32[32,8,128]{2,1,0:T(8,128)S(1)} %reduce_window_sum.22, f32[32,128,128]{2,1,0:T(8,128)S(1)} %fusion.35, pred[128,128]{1,0:T(8,128)(4,1)S(1)} %copy-done.11, bf16[32,128,8,64]{1,0,3,2:T(8,128)(2,1)S(1)} %bitcast.96), kind=kOutput, calls=%fused_computation.7 | convolution fusion | flops 562036736 | bytes 14958592 | tf_op jit(solution)/shard_map/chts,cshp->cthp/dot_general | solution.py:53
  201.3 7.6 %all-to-all-done = bf16[8,1,8,64,128]{4,3,2,1,0:T(8,128)(2,1)S(1)} async-done(((bf16[8,1,8,64,128]{4,3,2,1,0:T(8,128)(2,1)}), bf16[8,1,8,64,128]{4,3,2,1,0:T(8,128)(2,1)S(1)}, u32[]{:S(2)}, u32[]{:S(2)}) %all-to-all-start) | async-done | bytes 1048608 | tf_op jit(solution)/shard_map/all_to_all | solution.py:118
  208.9 1.3 fusion.24
  210.3 8.3 %fusion.9 = f32[32,128,8,64]{1,3,2,0:T(8,128)S(1)} fusion(f32[32,8,64,128]{3,2,1,0:T(8,128)} %fusion.1, f32[32,128,8,64]{1,3,2,0:T(8,128)} %fusion.36, f32[32,128,8]{1,2,0:T(8,128)S(1)} %copy-done.7, f32[32,128,8]{1,2,0:T(8,128)S(1)} %copy-done.6, bf16[32,128,128,1]{2,1,3,0:T(8,128)(2,1)S(1)} %bitcast.94, f32[8,64,128,1]{2,1,0,3:T(8,128)S(1)} %bitcast.100), kind=kOutput, calls=%fused_computation.21 | convolution fusion | flops 3229614080 | bytes 26738688 | tf_op jit(solution)/shard_map/ctn,hpn->cthp/dot_general | solution.py:131
  218.6 8.0 %copy.27 = f32[32,128,8,64]{1,0,3,2:T(8,128)} copy(f32[32,128,8,64]{1,3,2,0:T(8,128)S(1)} %fusion.9) | data formatting | bytes 16777216 | tf_op jit(solution)/shard_map/add | solution.py:132
  226.7 14.2 %multiply_reduce_fusion = (f32[4096]{0:T(1024)S(1)}, f32[4096,512]{0,1:T(8,128)S(1)}) fusion(bf16[4096,512]{0,1:T(8,128)(2,1)S(1)} %copy-done.4, f32[512]{0:T(512)S(1)} %copy-done.13, f32[64,8,32,128]{3,2,1,0:T(8,128)} %bitcast.91, f32[4099,512]{0,1:T(8,128)S(1)} %bitcast.90, f32[512]{0:T(512)S(1)} %bitcast.110, f32[512]{0:T(512)S(1)} %bitcast.108, ...), kind=kLoop, calls=%fused_computation.23 | loop fusion | flops 48230400 | bytes 54552576 | tf_op jit(solution)/shard_map/reduce_sum | solution.py:137
  242.6 3.2 %collective-permute-done.5 = f32[4096]{0:T(1024)S(1)} collective-permute-done((f32[4096]{0:T(1024)S(1)}, f32[4096]{0:T(1024)S(1)}, u32[]{:S(2)}, u32[]{:S(2)}) %collective-permute-start.5) | collective-permute-done | bytes 16416 | tf_op jit(solution)/shard_map/ppermute | solution.py:21
  245.9 3.3 %multiply_convert_fusion.2 = bf16[4096,512]{0,1:T(8,128)(2,1)} fusion(f32[4096,512]{0,1:T(8,128)S(1)} %get-tuple-element.69, f32[512]{0:T(512)S(1)} %copy-done.15, f32[4096]{0:T(1024)S(1)} %add_rsqrt_fusion), kind=kLoop, calls=%fused_computation.22 | loop fusion | flops 6291456 | bytes 12601344 | tf_op jit(solution)/shard_map/convert_element_type | solution.py:142
  249.2 6.4 %copy.29 = bf16[4096,512]{1,0:T(8,128)(2,1)} copy(bf16[4096,512]{0,1:T(8,128)(2,1)} %multiply_convert_fusion.2) | data formatting | bytes 8388608 | tf_op jit(solution)/shard_map/convert_element_type | solution.py:142
  (193 shorter events, 95.8 us)
Async XLA Ops:
  0.0 27.5 %copy-start.19 = (u32[256]{0:T(256)S(1)}, u32[256]{0:T(256)}, u32[]{:S(2)}) copy-start(u32[256]{0:T(256)} %constant.53) | copy-start | bytes 3076
  0.0 16.0 %copy-start.18 = (f32[8]{0:T(128)S(1)}, f32[8]{0:T(128)}, u32[]{:S(2)}) copy-start(f32[8]{0:T(128)} %param.17) | copy-start | bytes 100
  0.0 16.0 %copy-start.8 = (f32[4096,8]{0,1:T(8,128)S(1)}, f32[4096,8]{0,1:T(8,128)}, u32[]{:S(2)}) copy-start(f32[4096,8]{0,1:T(8,128)} %param.15) | copy-start | bytes 393220
  0.0 16.0 %copy-start.14 = (f32[8]{0:T(128)S(1)}, f32[8]{0:T(128)}, u32[]{:S(2)}) copy-start(f32[8]{0:T(128)} %param.16) | copy-start | bytes 100
  0.0 27.2 %copy-start.16 = (bf16[4,64]{1,0:T(4,128)(2,1)S(1)}, bf16[4,64]{1,0:T(4,128)(2,1)}, u32[]{:S(2)}) copy-start(bf16[4,64]{1,0:T(4,128)(2,1)} %param.20) | copy-start | bytes 1540
  0.0 27.2 %copy-start.12 = (bf16[4,512]{1,0:T(4,128)(2,1)S(1)}, bf16[4,512]{1,0:T(4,128)(2,1)}, u32[]{:S(2)}) copy-start(bf16[4,512]{1,0:T(4,128)(2,1)} %param.19) | copy-start | bytes 12292
  0.9 54.6 %collective-permute-start.1 = (bf16[3,64]{0,1:T(8,128)(2,1)S(1)}, bf16[3,64]{0,1:T(8,128)(2,1)S(1)}, u32[]{:S(2)}, u32[]{:S(2)}) collective-permute-start(bf16[3,64]{0,1:T(8,128)(2,1)S(1)} %slice.73), channel_id=1, source_target_pairs={{0,32},{32,64},{64,96},{96,128},{128,160},{160,192},{192,224},{1,3... | collective-permute-start | bytes 1160 | tf_op jit(solution)/shard_map/ppermute | solution.py:15
  5.6 51.2 %collective-permute-start = (bf16[3,512]{0,1:T(8,128)(2,1)S(1)}, bf16[3,512]{0,1:T(8,128)(2,1)S(1)}, u32[]{:S(2)}, u32[]{:S(2)}) collective-permute-start(bf16[3,512]{0,1:T(8,128)(2,1)S(1)} %copy.15), channel_id=1, source_target_pairs={{0,32},{32,64},{64,96},{96,128},{128,160},{160,192},{192,224},{1,3... | collective-permute-start | bytes 9224 | tf_op jit(solution)/shard_map/ppermute | solution.py:15
  9.5 45.4 %copy-start.17 = (f32[8]{0:T(128)S(1)}, f32[8]{0:T(128)}, u32[]{:S(2)}) copy-start(f32[8]{0:T(128)} %param.18) | copy-start | bytes 100
  9.5 46.0 %copy-start.5 = (bf16[4096,64]{0,1:T(8,128)(2,1)S(1)}, bf16[4096,64]{0,1:T(8,128)(2,1)}, u32[]{:S(2)}) copy-start(bf16[4096,64]{0,1:T(8,128)(2,1)} %param.14) | copy-start | bytes 1572868
  56.7 3.5 %collective-permute-start.2 = (bf16[4096,64]{0,1:T(8,128)(2,1)S(1)}, bf16[4096,64]{0,1:T(8,128)(2,1)S(1)}, u32[]{:S(2)}, u32[]{:S(2)}) collective-permute-start(bf16[4096,64]{0,1:T(8,128)(2,1)S(1)} %multiply_convert_fusion.5), channel_id=1, source_target_pairs={{0,1},{1,0},{2,3},{3,2},{4,5},{5,4},{6,7},{7,6},{8,9},{9,8},{10,11... | collective-permute-start | bytes 1572872 | tf_op jit(solution)/shard_map/ppermute | solution.py:21
  60.2 9.7 %copy-start = (f32[4099,512]{0,1:T(8,128)}, f32[4099,512]{0,1:T(8,128)S(1)}, u32[]{:S(2)}) copy-start(f32[4099,512]{0,1:T(8,128)S(1)} %maximum_convert_fusion) | copy-start | bytes 25184260
  60.5 24.9 %collective-permute-start.3 = (bf16[4096,128]{0,1:T(8,128)(2,1)S(1)}, bf16[4096,128]{0,1:T(8,128)(2,1)S(1)}, u32[]{:S(2)}, u32[]{:S(2)}) collective-permute-start(bf16[4096,128]{0,1:T(8,128)(2,1)S(1)} %maximum_select_fusion.1), channel_id=1, source_target_pairs={{0,2},{1,3},{2,0},{3,1},{4,6},{5,7},{6,4},{7,5},{8,10},{9,11},{10,... | collective-permute-start | bytes 3145736 | tf_op jit(solution)/shard_map/ppermute | solution.py:21
  73.4 12.7 %copy-start.2 = (bf16[64,8,32,128]{3,2,1,0:T(8,128)(2,1)}, bf16[64,8,32,128]{3,2,1,0:T(8,128)(2,1)S(1)}, u32[]{:S(2)}) copy-start(bf16[64,8,32,128]{3,2,1,0:T(8,128)(2,1)S(1)} %copy.37) | copy-start | bytes 12582916
  175.3 33.6 %all-to-all-start = ((bf16[8,1,8,64,128]{4,3,2,1,0:T(8,128)(2,1)}), bf16[8,1,8,64,128]{4,3,2,1,0:T(8,128)(2,1)S(1)}, u32[]{:S(2)}, u32[]{:S(2)}) async-start(bf16[8,1,8,64,128]{4,3,2,1,0:T(8,128)(2,1)} %stack.2), calls=%async_computation | async-start | bytes 2097152 | tf_op jit(solution)/shard_map/all_to_all | solution.py:118
  182.2 8.4 %copy-start.3 = (bf16[64,8,32,128]{3,2,1,0:T(8,128)(2,1)S(1)}, bf16[64,8,32,128]{3,2,1,0:T(8,128)(2,1)}, u32[]{:S(2)}) copy-start(bf16[64,8,32,128]{3,2,1,0:T(8,128)(2,1)} %copy-done.2) | copy-start | bytes 12582916
  190.6 18.3 %copy-start.10 = (f32[8,8,1,1]{0,2,3,1:T(1,128)S(1)}, f32[8,8,1,1]{0,2,3,1:T(1,128)}, u32[]{:S(2)}) copy-start(f32[8,8,1,1]{0,2,3,1:T(1,128)} %copy.32) | copy-start | bytes 772
  190.6 19.6 %copy-start.6 = (f32[32,128,8]{1,2,0:T(8,128)S(1)}, f32[32,128,8]{1,2,0:T(8,128)}, u32[]{:S(2)}) copy-start(f32[32,128,8]{1,2,0:T(8,128)} %get-tuple-element.76) | copy-start | bytes 393220
  190.6 19.6 %copy-start.7 = (f32[32,128,8]{1,2,0:T(8,128)S(1)}, f32[32,128,8]{1,2,0:T(8,128)}, u32[]{:S(2)}) copy-start(f32[32,128,8]{1,2,0:T(8,128)} %get-tuple-element.77) | copy-start | bytes 393220
  210.2 16.4 %slice-start = ((s8[8650752]{0:T(1024)(128)(4,1)}), s8[4194304]{0:T(1024)(128)(4,1)S(1)}, s32[]{:S(2)}) async-start(s8[8650752]{0:T(1024)(128)(4,1)} %bitcast.89), calls=%async_computation.1 | async-start | bytes 8388608
  210.3 16.4 %slice-start.1 = ((s8[8650752]{0:T(1024)(128)(4,1)}), s8[4194304]{0:T(1024)(128)(4,1)S(1)}, s32[]{:S(2)}) async-start(s8[8650752]{0:T(1024)(128)(4,1)} %bitcast.89), calls=%async_computation.2 | async-start | bytes 8388608
  226.7 19.2 %copy-start.15 = (f32[512]{0:T(512)S(1)}, f32[512]{0:T(512)}, u32[]{:S(2)}) copy-start(f32[512]{0:T(512)} %param.21) | copy-start | bytes 6148
  240.8 1.3 collective-permute-start.4
  242.1 3.7 %collective-permute-start.5 = (f32[4096]{0:T(1024)S(1)}, f32[4096]{0:T(1024)S(1)}, u32[]{:S(2)}, u32[]{:S(2)}) collective-permute-start(f32[4096]{0:T(1024)S(1)} %add.99), channel_id=1, source_target_pairs={{0,2},{1,3},{2,0},{3,1},{4,6},{5,7},{6,4},{7,5},{8,10},{9,11},{10,... | collective-permute-start | bytes 49160 | tf_op jit(solution)/shard_map/ppermute | solution.py:21
  (6 other events, 43.1 us)
